TPU v7x, 512 devices: a whole 4x4x16 slice. The times are simulated.
512 devices in a mesh: leaf: 16 (over z), col: 32 (over y, x, core).
Axes of the slice: x: 4, y: 4, z: 16, core: 2. Of those that a mesh axis runs over, the one named last changes fastest.
Arguments:
- leaf_solution: float32 [16, 16384, 256], P('leaf', 'col'), may hold values from -6 to 6
- coupling: float32 [16, 768, 128, 128], P('leaf', 'col'), may hold values from -0.01953125 to 0.01953125
- tile_slot: int32 [16, 768], P('leaf', 'col'), may hold values from 0 to 63, as said below
- sep_rhs: float32 [2048, 256], P('col'), may hold values from -6 to 6
- pivot_inverse: float32 [16, 128, 128], P('leaf'), as said below
Outputs:
- sep_solution: float32 [2048, 256], P('col')
- leaf_update: float32 [16, 16384, 256], P('leaf', 'col')
Inputs may be any that keep to these rules, and one draw needn't show every extreme that they name: `tile_slot`: within each aligned block of 24 entries along dimension 1 the values are distinct. `pivot_inverse`: each block is symmetric.
All inputs are finite; a program needn't handle non-finite values.
Results may differ from a plain program's by a relative error of at most 0.0003.
Values sent between devices are 32-bit elements; how exact they have to be, the bound alone decides.
No kernel may reach another device: no remote copies, remote signals or barrier semaphores. Data moves between devices by JAX's collectives and lax.ppermute only.
A program may use at most 64 MiB of HBM per device.

v0:
```python
import jax
import jax.numpy as jnp
from jax import lax
from jax.sharding import PartitionSpec as P


def on_device(leaf_solution, coupling, tile_slot, sep_rhs, pivot_inverse):
    precise = lax.Precision.HIGHEST
    tile_size = coupling.shape[-1]
    rhs_count = leaf_solution.shape[-1]
    leaf_rows = leaf_solution.shape[1]
    col_blocks = leaf_rows // tile_size
    own_rows = sep_rhs.shape[0]
    sep_rows = own_rows * lax.axis_size("col")
    row_blocks = sep_rows // tile_size
    tile_data = coupling[0]
    slot_ids = tile_slot[0]
    tile_row = slot_ids // col_blocks
    tile_col = slot_ids % col_blocks
    leaf_blocks = leaf_solution[0].reshape(col_blocks, tile_size, rhs_count)
    picked = leaf_blocks[tile_col]
    products = jnp.einsum("tij,tjk->tik", tile_data, picked, precision=precise)
    row_hot = (tile_row[None, :] == jnp.arange(row_blocks, dtype=jnp.int32)[:, None]).astype(
        jnp.float32
    )
    partial_value = -jnp.einsum("nt,tik->nik", row_hot, products, precision=precise).reshape(
        sep_rows, rhs_count
    )
    rhs_term = jnp.where(lax.axis_index("leaf") == 0, sep_rhs, jnp.zeros_like(sep_rhs))
    placed = lax.dynamic_update_slice_in_dim(
        jnp.zeros_like(partial_value), rhs_term, lax.axis_index("col") * own_rows, 0
    )
    partial_value = partial_value + placed
    summed = lax.psum(partial_value, ("leaf", "col"))
    pivots = lax.all_gather(pivot_inverse, "leaf", axis=0, tiled=True)
    solved = jnp.einsum(
        "bij,bjk->bik", pivots, summed.reshape(row_blocks, tile_size, rhs_count), precision=precise
    )
    solution = solved.reshape(sep_rows, rhs_count)
    sep_blocks = solution.reshape(row_blocks, tile_size, rhs_count)
    chosen = sep_blocks[tile_row]
    transposed = jnp.einsum("tij,tik->tjk", tile_data, chosen, precision=precise)
    col_hot = (tile_col[None, :] == jnp.arange(col_blocks, dtype=jnp.int32)[:, None]).astype(
        jnp.float32
    )
    update = jnp.einsum("ct,tjk->cjk", col_hot, transposed, precision=precise)
    leaf_update = (leaf_blocks - update).reshape(1, leaf_rows, rhs_count)
    sep_solution = lax.dynamic_slice_in_dim(solution, lax.axis_index("col") * own_rows, own_rows, 0)
    return (sep_solution, leaf_update)


def solution(mesh):
    return jax.shard_map(
        on_device,
        mesh=mesh,
        in_specs=(
            P("leaf", "col", None),
            P("leaf", "col", None, None),
            P("leaf", "col"),
            P("col", None),
            P("leaf", None, None),
        ),
        out_specs=(P("col", None), P("leaf", "col", None)),
        check_vma=False,
    )
```

profile of v0, /device:TPU:1, one launch (start us, length us, event | category | flops | bytes accessed | tf_op | source)
XLA Modules:
  0.0 554.2 jit_solution(7920181868726836255)
XLA Ops:
  8.0 0.0 copy-start
  8.0 0.0 all-reduce.2.cloned.1.call-start
  8.1 0.8 fusion.11
  8.8 0.7 fusion.9
  9.5 3.5 gather_fusion
  13.0 0.0 copy-done
  13.0 8.3 %convolution_bitcast_fusion.1 = f32[24,128,256]{1,2,0:T(8,128)} fusion(f32[24,128,256]{2,1,0:T(8,128)} %gather_fusion, f32[1,24,128,128]{3,2,1,0:T(8,128)S(1)} %copy-done), kind=kOutput, calls=%fused_computation.3 | convolution fusion | flops 1207959552 | bytes 7864320 | tf_op jit(solution)/shard_map/tij,tjk->tik/dot_general | solution.py:22
  21.3 3.6 copy.18
  24.8 3.3 convolution_negate_fusion
  28.1 0.0 copy-start.3
  28.1 2.5 copy.19
  30.6 0.0 copy-done.3
  30.6 1.5 add_dynamic-update-slice_fusion
  32.1 0.0 all-reduce.2.cloned.1.call-update
  32.1 0.2 all-gather.2.cloned.1.call-start
  32.4 0.3 all-gather.2.cloned.1.call-update
  32.7 488.4 %all-reduce.2.cloned.1.call-done = f32[16,128,256]{2,1,0:T(8,128)} async-done(((f32[16,128,256]{2,1,0:T(8,128)}), f32[16,128,256]{2,1,0:T(8,128)}) %all-reduce.2.cloned.1.call-update) | async-done | bytes 2097168 | tf_op jit(solution)/shard_map/psum | solution.py:34
  521.1 0.0 all-gather.2.cloned.1.call-done
  521.1 3.8 fusion.13
  525.0 0.0 copy-start.2
  525.0 1.3 copy-done.2
  526.3 0.6 constant_dynamic-slice_fusion
  526.9 4.0 gather_fusion.1
  530.9 8.3 %convolution_bitcast_fusion = f32[24,128,256]{1,2,0:T(8,128)} fusion(f32[24,128,256]{2,1,0:T(8,128)} %gather_fusion.1, f32[1,24,128,128]{3,2,1,0:T(8,128)S(1)} %copy-done), kind=kOutput, calls=%fused_computation.2 | convolution fusion | flops 1207959552 | bytes 7864320 | tf_op jit(solution)/shard_map/tij,tik->tjk/dot_general | solution.py:42
  539.2 3.6 copy.21
  542.7 0.0 copy-start.1
  542.7 3.2 fusion.6
  545.9 0.0 copy-done.1
  545.9 0.9 copy_subtract_fusion
  (2 shorter events, 0.0 us)
Async XLA Ops:
  8.0 5.0 copy-start
  8.0 513.1 %all-reduce.2.cloned.1.call-start = ((), (), s32[]{:S(2)}) async-start(), calls=%async_computation | async-start | bytes 4194304 | tf_op jit(solution)/shard_map/psum | solution.py:34
  28.1 2.5 copy-start.3
  32.1 489.0 %all-gather.2.cloned.1.call-start = ((), (), s32[]{:S(2)}) async-start(), calls=%async_computation.1 | async-start | bytes 1114112 | tf_op jit(solution)/shard_map/all_gather | solution.py:35
  525.0 1.3 copy-start.2
  542.7 3.2 copy-start.1
Sparse Core Ops, SparseCore 0:
  32.3 488.7 all-reduce.1
Sparse Core Ops, SparseCore 1:
  34.7 66.8 all-gather.1
where the time goes:
time: 555 us; the launch traced here: 554 us
  waiting for transfers between devices  489 us (88%)
  matrix products  26.8 us (5%)
  local copies, waits for them, and re-layouts  19.1 us (3%)
  between operations  15.5 us (3%)
    psum x1, waiting for transfers between devices, on_device(): summed = lax.psum(partial_value, ('leaf', 'col'))  488 us
  transfers between devices with their start and end apart: 2, of which 1 were waited for; matrix products, arithmetic and copies ran while one was open for 0% of the time, Pallas kernels for 0%

commit v1 on v0

--- a/solution.py
+++ b/solution.py
@@ -31,7 +31,7 @@
         jnp.zeros_like(partial_value), rhs_term, lax.axis_index("col") * own_rows, 0
     )
     partial_value = partial_value + placed
-    summed = lax.psum(partial_value, ("leaf", "col"))
+    summed = lax.psum(lax.psum(partial_value, "leaf"), "col")
     pivots = lax.all_gather(pivot_inverse, "leaf", axis=0, tiled=True)
     solved = jnp.einsum(
         "bij,bjk->bik", pivots, summed.reshape(row_blocks, tile_size, rhs_count), precision=precise

time: 555 us -> 422 us (0.76)
  waiting for transfers between devices: 489 us -> 358 us
    psum x1 -> x2, waiting for transfers between devices: 488 us -> 288 us  [on_device(): summed = lax.psum(lax.psum(partial_value, 'leaf'), 'col')]
    all_gather x1, waiting for transfers between devices: 0.01 us -> 68.8 us  [on_device(): pivots = lax.all_gather(pivot_inverse, 'leaf', axis=0, tiled=True)]
  transfers between devices with their start and end apart: 2 -> 3, of which waited for: 1 -> 3; matrix products, arithmetic and copies ran while one was open for 0% -> 0% of each run, Pallas kernels for 0% -> 0%
where the time goes in v1:
time: 422 us; the launch traced here: 421 us
  waiting for transfers between devices  358 us (85%)
  matrix products  26.8 us (6%)
  local copies, waits for them, and re-layouts  19.1 us (5%)
  between operations  13.8 us (3%)
    psum x2, waiting for transfers between devices, on_device(): summed = lax.psum(lax.psum(partial_value, 'leaf'), 'col')  288 us
    all_gather x1, waiting for transfers between devices, on_device(): pivots = lax.all_gather(pivot_inverse, 'leaf', axis=0, tiled=True)  68.8 us
  transfers between devices with their start and end apart: 3, of which 3 were waited for; matrix products, arithmetic and copies ran while one was open for 0% of the time, Pallas kernels for 0%

profile of v1, /device:TPU:1, one launch (start us, length us, event | category | flops | bytes accessed | tf_op | source)
XLA Modules:
  0.0 421.5 jit_solution(17871048465799552161)
XLA Ops:
  7.2 0.0 copy-start
  7.2 0.0 all-reduce.3.cloned.1.call-start
  7.2 0.8 fusion.11
  8.0 0.7 fusion.9
  8.7 3.5 gather_fusion
  12.2 0.0 copy-done
  12.2 8.3 %convolution_bitcast_fusion.1 = f32[24,128,256]{1,2,0:T(8,128)} fusion(f32[24,128,256]{2,1,0:T(8,128)} %gather_fusion, f32[1,24,128,128]{3,2,1,0:T(8,128)S(1)} %copy-done), kind=kOutput, calls=%fused_computation.3 | convolution fusion | flops 1207959552 | bytes 7864320 | tf_op jit(solution)/shard_map/tij,tjk->tik/dot_general | solution.py:22
  20.4 3.6 copy.18
  24.0 3.3 convolution_negate_fusion
  27.3 0.0 copy-start.3
  27.3 2.5 copy.19
  29.8 0.0 copy-done.3
  29.8 1.5 add_dynamic-update-slice_fusion
  31.3 0.0 all-reduce.3.cloned.1.call-update
  31.3 0.0 all-gather.2.cloned.1.call-start
  31.4 0.7 all-gather.2.cloned.1.call-update
  32.1 0.2 all-reduce.5.cloned.1.call-start
  32.3 139.3 %all-reduce.3.cloned.1.call-done = f32[2048,256]{1,0:T(8,128)} async-done(((f32[2048,256]{1,0:T(8,128)}), f32[2048,256]{1,0:T(8,128)}) %all-reduce.3.cloned.1.call-update) | async-done | bytes 2097168 | tf_op jit(solution)/shard_map/psum | solution.py:34
  171.6 0.0 all-reduce.5.cloned.1.call-update
  171.7 68.8 %all-gather.2.cloned.1.call-done = f32[16,128,128]{2,1,0:T(8,128)} async-done(((f32[1,128,128]{2,1,0:T(8,128)}), f32[16,128,128]{2,1,0:T(8,128)}) %all-gather.2.cloned.1.call-update) | async-done | bytes 1048592 | tf_op jit(solution)/shard_map/all_gather | solution.py:35
  240.4 148.8 %all-reduce.5.cloned.1.call-done = f32[16,128,256]{2,1,0:T(8,128)} async-done(((f32[16,128,256]{2,1,0:T(8,128)}), f32[16,128,256]{2,1,0:T(8,128)}) %all-reduce.5.cloned.1.call-update) | async-done | bytes 2097168 | tf_op jit(solution)/shard_map/psum | solution.py:34
  389.2 3.8 fusion.13
  393.1 0.0 copy-start.2
  393.1 1.3 copy-done.2
  394.4 0.6 constant_dynamic-slice_fusion
  395.1 4.0 gather_fusion.1
  399.0 8.3 %convolution_bitcast_fusion = f32[24,128,256]{1,2,0:T(8,128)} fusion(f32[24,128,256]{2,1,0:T(8,128)} %gather_fusion.1, f32[1,24,128,128]{3,2,1,0:T(8,128)S(1)} %copy-done), kind=kOutput, calls=%fused_computation.2 | convolution fusion | flops 1207959552 | bytes 7864320 | tf_op jit(solution)/shard_map/tij,tik->tjk/dot_general | solution.py:42
  407.3 3.6 copy.21
  410.8 0.0 copy-start.1
  410.9 3.2 fusion.6
  414.0 0.0 copy-done.1
  414.0 0.9 copy_subtract_fusion
  (2 shorter events, 0.0 us)
Async XLA Ops:
  7.2 5.0 %copy-start = (f32[1,24,128,128]{3,2,1,0:T(8,128)S(1)}, f32[1,24,128,128]{3,2,1,0:T(8,128)}, u32[]{:S(2)}) copy-start(f32[1,24,128,128]{3,2,1,0:T(8,128)} %param.6) | copy-start | bytes 4718596
  7.2 164.4 %all-reduce.3.cloned.1.call-start = ((), (), s32[]{:S(2)}) async-start(), calls=%async_computation | async-start | bytes 4194304 | tf_op jit(solution)/shard_map/psum | solution.py:34
  27.3 2.5 copy-start.3
  31.3 209.1 %all-gather.2.cloned.1.call-start = ((), (), s32[]{:S(2)}) async-start(), calls=%async_computation.2 | async-start | bytes 1114112 | tf_op jit(solution)/shard_map/all_gather | solution.py:35
  32.1 357.2 %all-reduce.5.cloned.1.call-start = ((), (), s32[]{:S(2)}) async-start(), calls=%async_computation.1 | async-start | bytes 4194304 | tf_op jit(solution)/shard_map/psum | solution.py:34
  393.1 1.3 copy-start.2
  410.8 3.2 copy-start.1
Sparse Core Ops, SparseCore 0:
  31.4 140.1 all-reduce.2
  173.7 66.6 all-gather.1
  243.7 145.5 all-reduce.4
